TPU v7x, 512 devices: a whole 4x4x16 slice. The times are simulated.
512 devices in a mesh: seq: 32 (over z, core), dp: 16 (over x, y).
Axes of the slice: x: 4, y: 4, z: 16, core: 2. Of those that a mesh axis runs over, the one named last changes fastest.
Arguments:
- queries: bfloat16 [16, 5120, 2048], P('dp', 'seq'), may hold values from -6 to 6
- keys: bfloat16 [16, 5120, 2048], P('dp', 'seq'), may hold values from -6 to 6
- values: bfloat16 [16, 5120, 2048], P('dp', 'seq'), may hold values from -6 to 6
- keep: int32 [16, 5120, 2048], P('dp', 'seq'), may hold values 0 or 1
- gain: float32 [2048], replicated, may hold values from 0.25 to 1.75
- out_weight: bfloat16 [2048, 2048], P(None, 'dp'), may hold values from -0.125 to 0.125
Outputs:
- projected: bfloat16 [16, 5120, 2048], P('dp', 'seq')
All inputs are finite; a program needn't handle non-finite values. No bound on the sum of `keep` on one device may be relied on, other than what follows from the above.
Results may differ from a plain program's by a relative error of at most 0.0051.
Values may be sent and summed in bfloat16 or wider, within the bound.
No kernel may reach another device: no remote copies, remote signals or barrier semaphores. Data moves between devices by JAX's collectives and lax.ppermute only.
A program may use at most 128 MiB of HBM per device.

v0:
```python
import jax
import jax.numpy as jnp
from jax import lax
from jax.sharding import PartitionSpec as P

HEADS = 16
HEAD = 128


def prefix_2(x, axis, combine, identity):
    size, place = (lax.axis_size(axis), lax.axis_index(axis))
    everything = lax.all_gather(x, axis)
    start = jnp.broadcast_to(jnp.asarray(identity, x.dtype), x.shape)

    def turn(k, before):
        reached = k < place
        new = combine(before, everything[k])
        return jnp.where(reached, new, before)

    return lax.fori_loop(0, size, turn, start)


def feature(x):
    xf = x.astype(jnp.float32)
    return jnp.where(xf > 0, xf + 1.0, jnp.exp(jnp.minimum(xf, 0.0))).astype(jnp.bfloat16)


def add_states(earlier, later):
    return earlier + later


def on_device(queries, keys, values, keep, gain, out_weight):
    tok_rows = queries.shape[1]
    fq = feature(queries[0]).reshape(tok_rows, HEADS, HEAD)
    fk = feature(keys[0]).reshape(tok_rows, HEADS, HEAD)
    vals = values[0].reshape(tok_rows, HEADS, HEAD)
    state = jnp.einsum("thc,thd->hcd", fk, vals, preferred_element_type=jnp.float32)
    prefix = prefix_2(state, "seq", add_states, jnp.zeros_like(state))
    prefix = prefix.astype(jnp.bfloat16)
    inter = jnp.einsum("thc,hcd->thd", fq, prefix, preferred_element_type=jnp.float32)
    causal = jnp.arange(tok_rows)[:, None] >= jnp.arange(tok_rows)[None, :]
    scores = jnp.einsum("thc,shc->hts", fq, fk, preferred_element_type=jnp.float32)
    scores = jnp.where(causal[None], scores, 0.0).astype(jnp.bfloat16)
    intra = jnp.einsum("hts,shd->thd", scores, vals, preferred_element_type=jnp.float32)
    numer = inter + intra
    normed = (
        numer
        * lax.rsqrt(jnp.mean(numer * numer, axis=-1, keepdims=True) + 1e-06)
        * gain.reshape(HEADS, HEAD)
    )
    mask = keep[0].reshape(tok_rows, HEADS, HEAD).astype(jnp.float32)
    dropped = (normed * mask * (1.0 / 0.9)).astype(jnp.bfloat16).reshape(tok_rows, HEADS * HEAD)
    result = jnp.dot(
        dropped,
        lax.all_gather(out_weight, "dp", axis=1, tiled=True),
        preferred_element_type=jnp.float32,
    ).astype(jnp.bfloat16)
    return result[None]


def solution(mesh):
    return jax.shard_map(
        on_device,
        mesh=mesh,
        in_specs=(
            P("dp", "seq", None),
            P("dp", "seq", None),
            P("dp", "seq", None),
            P("dp", "seq", None),
            P(),
            P(None, "dp"),
        ),
        out_specs=P("dp", "seq", None),
        check_vma=False,
    )
```

profile of v0, /device:TPU:2, one launch (start us, length us, event | category | flops | bytes accessed | tf_op | source)
XLA Modules:
  0.0 313.0 jit_solution(7465845264773032418)
XLA Ops:
  14.4 3.3 %fusion.3 = f32[160,16,128]{2,0,1:T(8,128)} fusion(pred[160,160]{1,0:T(8,128)(4,1)S(1)} %iota_compare_fusion, bf16[160,16,128]{2,1,0:T(8,128)(2,1)} %bitcast.42, bf16[160,16,128]{2,1,0:T(8,128)(2,1)} %bitcast.41, bf16[160,16,128]{2,1,0:T(8,128)(2,1)S(1)} %bitcast.39), kind=kOutput, calls=%fused_computation.13 | convolution fusion | flops 210534400 | bytes 3302400 | tf_op jit(solution)/shard_map/hts,shd->thd/dot_general | solution.py:44
  17.7 188.8 %all-gather.6.cloned.1.call-done = f32[512,128,128]{2,1,0:T(8,128)} async-done(((f32[16,128,128]{2,1,0:T(8,128)}), f32[512,128,128]{2,1,0:T(8,128)}) %all-gather.6.cloned.1.call-update) | async-done | bytes 33554448 | tf_op jit(solution)/shard_map/all_gather | solution.py:12
  206.5 51.9 %while.14 = (s32[]{:T(128)}, f32[16,128,128]{2,1,0:T(8,128)S(1)}, s32[]{:T(128)}, f32[32,16,128,128]{3,2,1,0:T(8,128)}, s32[]{:T(128)}, /*index=5*/s32[]{:T(128)}) while((s32[]{:T(128)}, f32[16,128,128]{2,1,0:T(8,128)S(1)}, s32[]{:T(128)}, f32[32,16,128,128]{3,2,1,0:T(8,128)}, s32[]{:T(128)}, /*index=5*/s32[]{:T(128)}) %tuple.40), condition=%wide.region_1.2_spmd.clone, body=%wide.region_0.1_spmd.clone.sunk | while | flops 786436 | bytes 3145821 | solution.py:20
  206.5 1.7 add_select_fusion.2
  208.2 1.6 add_select_fusion.2
  209.8 1.6 add_select_fusion.2
  211.4 1.6 add_select_fusion.2
  213.0 1.6 add_select_fusion.2
  214.6 1.6 add_select_fusion.2
  216.2 1.6 add_select_fusion.2
  217.8 1.6 add_select_fusion.2
  221.1 1.6 add_select_fusion.2
  222.7 1.6 add_select_fusion.2
  224.3 1.7 add_select_fusion.2
  226.0 1.6 add_select_fusion.2
  227.7 1.6 add_select_fusion.2
  229.3 1.6 add_select_fusion.2
  230.9 1.6 add_select_fusion.2
  232.5 1.6 add_select_fusion.2
  234.1 1.6 add_select_fusion.2
  235.8 1.6 add_select_fusion.2
  237.4 1.6 add_select_fusion.2
  242.2 1.6 add_select_fusion.2
  243.9 1.6 add_select_fusion.2
  245.5 1.6 add_select_fusion.2
  250.3 1.6 add_select_fusion.2
  251.9 1.6 add_select_fusion.2
  253.5 1.6 add_select_fusion.2
  256.8 1.6 add_select_fusion.2
  258.4 3.1 multiply_reduce_fusion
  261.5 38.1 %all-gather.4.cloned.1.call-done = bf16[2048,2048]{1,0:T(8,128)(2,1)} async-done(((bf16[2048,128]{1,0:T(8,128)(2,1)}), bf16[2048,2048]{1,0:T(8,128)(2,1)}) %all-gather.4.cloned.1.call-update) | async-done | bytes 8388624 | tf_op jit(solution)/shard_map/all_gather | solution.py:55
  299.6 6.6 %fusion = bf16[1,160,2048]{2,1,0:T(8,128)(2,1)} fusion(bf16[2048,2048]{1,0:T(8,128)(2,1)} %all-gather.4.cloned.1.call-done, f32[160,16,128]{2,1,0:T(8,128)S(1)} %bitcast.37, f32[160,16,128]{2,0,1:T(8,128)} %get-tuple-element.109, f32[16,128]{1,0:T(8,128)S(1)} %bitcast.46, f32[160,16]{0,1:T(8,128)S(1)} %add_rsqrt_fusion), kind=kOutput, calls=%fused_computation.3 | convolution fusion | flops 1344143360 | bytes 11683840 | tf_op jit(solution)/shard_map/dot_general | solution.py:53
  (31 shorter events, 17.3 us)
Async XLA Ops:
  6.5 1.6 copy-start.3
  6.5 199.9 %all-gather.6.cloned.1.call-start = ((), (), s32[]{:S(2)}) async-start(), calls=%async_computation.1 | async-start | bytes 34603008 | tf_op jit(solution)/shard_map/all_gather | solution.py:12
  8.3 0.9 copy-start
  10.7 288.9 %all-gather.4.cloned.1.call-start = ((), (), s32[]{:S(2)}) async-start(), calls=%async_computation | async-start | bytes 8912896 | tf_op jit(solution)/shard_map/all_gather | solution.py:55
  11.5 2.5 copy-start.2
  206.5 51.9 %copy-start.1 = (bf16[20,8,16,128]{3,2,1,0:T(8,128)(2,1)S(1)}, bf16[20,8,16,128]{3,2,1,0:T(8,128)(2,1)}, u32[]{:S(2)}) copy-start(bf16[20,8,16,128]{3,2,1,0:T(8,128)(2,1)} %copy.26) | copy-start | bytes 1966084
  258.4 41.2 %copy-start.4 = (f32[2048]{0:T(1024)S(1)}, f32[2048]{0:T(1024)}, u32[]{:S(2)}) copy-start(f32[2048]{0:T(1024)} %param.12) | copy-start | bytes 24580
Sparse Core Ops, SparseCore 0:
  10.8 195.6 all-gather.5
  209.5 90.0 all-gather.3
where the time goes:
time: 314 us; the launch traced here: 313 us
  waiting for transfers between devices  228 us (73%)
  other arithmetic  54.3 us (17%)
  matrix products  14.4 us (5%)
  between operations  13.5 us (4%)
    all_gather x1, waiting for transfers between devices, prefix_2(): everything = lax.all_gather(x, axis)  189 us
    select_n x32, other arithmetic, turn(): return jnp.where(reached, new, before)  51.1 us
    all_gather x1, waiting for transfers between devices, on_device(): lax.all_gather(out_weight, 'dp', axis=1, tiled=True)  38.1 us
    dot_general x1, matrix products, on_device(): jnp.dot(dropped, lax.all_gather(out_weight, 'dp', axis=1, tiled=True), pr...  6.56 us
  transfers between devices with their start and end apart: 2, of which 2 were waited for; matrix products, arithmetic and copies ran while one was open for 19% of the time, Pallas kernels for 0%

commit v1 on v0

--- a/solution.py
+++ b/solution.py
@@ -52,7 +52,9 @@
     dropped = (normed * mask * (1.0 / 0.9)).astype(jnp.bfloat16).reshape(tok_rows, HEADS * HEAD)
     result = jnp.dot(
         dropped,
-        lax.all_gather(out_weight, "dp", axis=1, tiled=True),
+        jnp.concatenate(
+            lax.all_to_all(jnp.stack([out_weight] * lax.axis_size("dp")), "dp", 0, 0), axis=1
+        ),
         preferred_element_type=jnp.float32,
     ).astype(jnp.bfloat16)
     return result[None]

time: 314 us -> 278 us (0.89)
  the two profiles are of different devices: /device:TPU:2 before, /device:TPU:1 now
where the time goes in v1:
time: 278 us; the launch traced here: 277 us
  waiting for transfers between devices  178 us (64%)
  other arithmetic  54.2 us (19%)
  matrix products  15.4 us (6%)
  between operations  13.5 us (5%)
  starting transfers between devices  7.76 us (3%)
  local copies, waits for them, and re-layouts  6.85 us (2%)
    all_gather x1, waiting for transfers between devices, prefix_2(): everything = lax.all_gather(x, axis)  178 us
    select_n x32, other arithmetic, turn(): return jnp.where(reached, new, before)  50.9 us
    all_to_all x1, starting transfers between devices, on_device(): lax.all_to_all(jnp.stack([out_weight] * lax.axis_size('dp')), 'dp', 0, 0)  7.76 us
    dot_general x1, matrix products, on_device(): jnp.dot(dropped, jnp.concatenate(lax.all_to_all(jnp.stack([out_weight] *...  7.64 us
  transfers between devices with their start and end apart: 2, of which 1 were waited for; matrix products, arithmetic and copies ran while one was open for 23% of the time, Pallas kernels for 0%

profile of v1, /device:TPU:1, one launch (start us, length us, event | category | flops | bytes accessed | tf_op | source)
XLA Modules:
  0.0 277.0 jit_solution(3450503509679357759)
XLA Ops:
  10.9 4.3 %stack.2 = bf16[16,2048,128]{1,2,0:T(8,128)(2,1)} broadcast(bf16[2048,128]{0,1:T(8,128)(2,1)S(1)} %copy.26), dimensions={1,2} | broadcast | bytes 8912896 | tf_op jit(solution)/shard_map/stack | solution.py:56
  15.2 7.8 %all-to-all-start = ((bf16[16,2048,128]{1,2,0:T(8,128)(2,1)}), bf16[16,2048,128]{1,2,0:T(8,128)(2,1)}, u32[]{:S(2)}, u32[]{:S(2)}) async-start(bf16[16,2048,128]{1,2,0:T(8,128)(2,1)} %stack.2), calls=%async_computation | async-start | bytes 16777216 | tf_op jit(solution)/shard_map/all_to_all | solution.py:56
  26.0 3.3 %fusion.3 = f32[160,16,128]{2,0,1:T(8,128)} fusion(pred[160,160]{1,0:T(8,128)(4,1)S(1)} %iota_compare_fusion, bf16[160,16,128]{2,1,0:T(8,128)(2,1)} %bitcast.45, bf16[160,16,128]{2,1,0:T(8,128)(2,1)} %bitcast.44, bf16[160,16,128]{2,1,0:T(8,128)(2,1)S(1)} %bitcast.42), kind=kOutput, calls=%fused_computation.13 | convolution fusion | flops 210534400 | bytes 3302400 | tf_op jit(solution)/shard_map/hts,shd->thd/dot_general | solution.py:44
  29.3 178.4 %all-gather.3.cloned.1.call-done = f32[512,128,128]{2,1,0:T(8,128)} async-done(((f32[16,128,128]{2,1,0:T(8,128)}), f32[512,128,128]{2,1,0:T(8,128)}) %all-gather.3.cloned.1.call-update) | async-done | bytes 33554448 | tf_op jit(solution)/shard_map/all_gather | solution.py:12
  207.7 51.7 %while.14 = (s32[]{:T(128)}, f32[16,128,128]{2,1,0:T(8,128)S(1)}, s32[]{:T(128)}, f32[32,16,128,128]{3,2,1,0:T(8,128)}, s32[]{:T(128)}, /*index=5*/s32[]{:T(128)}) while((s32[]{:T(128)}, f32[16,128,128]{2,1,0:T(8,128)S(1)}, s32[]{:T(128)}, f32[32,16,128,128]{3,2,1,0:T(8,128)}, s32[]{:T(128)}, /*index=5*/s32[]{:T(128)}) %tuple.38), condition=%wide.region_1.2_spmd.clone, body=%wide.region_0.1_spmd.clone.sunk | while | flops 786436 | bytes 3145821 | solution.py:20
  207.7 1.7 add_select_fusion.2
  209.4 1.6 add_select_fusion.2
  211.0 1.6 add_select_fusion.2
  212.6 1.6 add_select_fusion.2
  214.2 1.6 add_select_fusion.2
  215.8 1.6 add_select_fusion.2
  217.5 1.6 add_select_fusion.2
  219.1 1.6 add_select_fusion.2
  220.7 1.6 add_select_fusion.2
  222.3 1.6 add_select_fusion.2
  223.9 1.6 add_select_fusion.2
  225.5 1.6 add_select_fusion.2
  230.4 1.6 add_select_fusion.2
  232.0 1.6 add_select_fusion.2
  233.6 1.6 add_select_fusion.2
  236.8 1.6 add_select_fusion.2
  238.4 1.6 add_select_fusion.2
  240.0 1.6 add_select_fusion.2
  241.7 1.6 add_select_fusion.2
  244.9 1.6 add_select_fusion.2
  246.5 1.6 add_select_fusion.2
  248.1 1.6 add_select_fusion.2
  253.0 1.6 add_select_fusion.2
  254.6 1.6 add_select_fusion.2
  256.2 1.6 add_select_fusion.2
  259.4 3.0 %multiply_reduce_fusion = (f32[160,16]{0,1:T(8,128)S(1)}, f32[160,16,128]{2,0,1:T(8,128)}) fusion(f32[160,16,128]{2,0,1:T(8,128)} %fusion.3, f32[16,128,128]{2,1,0:T(8,128)S(1)} %get-tuple-element.84, bf16[160,16,128]{2,1,0:T(8,128)(2,1)S(1)} %bitcast.46), kind=kOutput, calls=%fused_computation.24 | convolution fusion | flops 85128704 | bytes 4335616 | tf_op jit(solution)/shard_map/thc,hcd->thd/dot_general | solution.py:40
  262.5 7.6 %fusion = bf16[1,160,2048]{2,1,0:T(8,128)(2,1)} fusion(bf16[2048,2048]{0,1:T(8,128)(2,1)} %bitcast.5, f32[160,16,128]{2,1,0:T(8,128)S(1)} %bitcast.40, f32[160,16,128]{2,0,1:T(8,128)} %get-tuple-element.109, f32[16,128]{1,0:T(8,128)S(1)} %bitcast.49, f32[160,16]{0,1:T(8,128)S(1)} %add_rsqrt_fusion), kind=kOutput, calls=%fused_computation.3 | convolution fusion | flops 1344143360 | bytes 11683840 | tf_op jit(solution)/shard_map/dot_general | solution.py:53
  (34 shorter events, 18.4 us)
Async XLA Ops:
  6.5 1.6 copy-start.2
  6.5 201.2 %all-gather.3.cloned.1.call-start = ((), (), s32[]{:S(2)}) async-start(), calls=%async_computation.1 | async-start | bytes 34603008 | tf_op jit(solution)/shard_map/all_gather | solution.py:12
  8.3 0.8 copy-start
  9.2 1.5 copy-start.4
  15.2 7.8 %copy-start.3 = (bf16[1,160,2048]{2,1,0:T(8,128)(2,1)S(1)}, bf16[1,160,2048]{2,1,0:T(8,128)(2,1)}, u32[]{:S(2)}) copy-start(bf16[1,160,2048]{2,1,0:T(8,128)(2,1)} %param.8) | copy-start | bytes 1966084
  15.2 247.2 %all-to-all-start = ((bf16[16,2048,128]{1,2,0:T(8,128)(2,1)}), bf16[16,2048,128]{1,2,0:T(8,128)(2,1)}, u32[]{:S(2)}, u32[]{:S(2)}) async-start(bf16[16,2048,128]{1,2,0:T(8,128)(2,1)} %stack.2), calls=%async_computation | async-start | bytes 16777216 | tf_op jit(solution)/shard_map/all_to_all | solution.py:56
  207.7 51.7 %copy-start.1 = (bf16[20,8,16,128]{3,2,1,0:T(8,128)(2,1)S(1)}, bf16[20,8,16,128]{3,2,1,0:T(8,128)(2,1)}, u32[]{:S(2)}) copy-start(bf16[20,8,16,128]{3,2,1,0:T(8,128)(2,1)} %copy.28) | copy-start | bytes 1966084
  259.4 3.1 %copy-start.5 = (f32[2048]{0:T(1024)S(1)}, f32[2048]{0:T(1024)}, u32[]{:S(2)}) copy-start(f32[2048]{0:T(1024)} %param.12) | copy-start | bytes 24580
Sparse Core Ops, SparseCore 0:
  10.8 196.8 all-gather.2
